TPU v7x, 32 devices: a whole 2x2x4 slice. The times are simulated.
32 devices in a mesh: tm: 8 (over z, x), lon: 4 (over y, core).
Axes of the slice: x: 2, y: 2, z: 4, core: 2. Of those that a mesh axis runs over, the one named last changes fastest.
Arguments:
- start: float32 [3, 128, 512], P(None, 'lon'), may hold values from -6 to 6
- depth: float32 [128, 512], P('lon'), may hold values from 0.5 to 1.5
Outputs:
- ends: float32 [8, 3, 128, 512], P('tm', None, 'lon')
All inputs are finite; a program needn't handle non-finite values.
Results may differ from a plain program's by a relative error of at most 0.00002.
Values sent between devices are 32-bit elements; how exact they have to be, the bound alone decides.
No kernel may reach another device: no remote copies, remote signals or barrier semaphores. Data moves between devices by JAX's collectives and lax.ppermute only.
A program may use at most 64 MiB of HBM per device.

v0:
```python
import math

import jax
import jax.numpy as jnp
from jax import lax
from jax.sharding import PartitionSpec as P

STEPS = 3
ROUNDS = 2


LAT_LIMIT = 1.2
COURANT = 1.2
DEPTH_MAX = 1.5
GRAVITY = 1.0
TURN_RATE = 0.15


def padded_2(cells, sides, width):
    for axis, dim in sides:
        count = lax.axis_size(axis)
        head = lax.slice_in_dim(cells, 0, width, axis=dim)
        tail = lax.slice_in_dim(cells, cells.shape[dim] - width, cells.shape[dim], axis=dim)
        cells = jnp.concatenate(
            [
                lax.ppermute(tail, axis, [(i, (i + 1) % count) for i in range(count)]),
                cells,
                lax.ppermute(head, axis, [((i + 1) % count, i) for i in range(count)]),
            ],
            axis=dim,
        )
    return cells


def grid_constants(lon_cells, lat_cells):
    latitude = -LAT_LIMIT + (jnp.arange(lat_cells, dtype=jnp.float32) + 0.5) * (
        2.0 * LAT_LIMIT / lat_cells
    )
    cosine = jnp.cos(latitude)
    north_spacing = 2.0 * LAT_LIMIT / lat_cells
    east_spacing = cosine * (2.0 * math.pi / lon_cells)
    narrowest = math.cos(LAT_LIMIT - LAT_LIMIT / lat_cells) * 2.0 * math.pi / lon_cells
    time_step = COURANT / (
        math.sqrt(DEPTH_MAX * GRAVITY) * math.sqrt(1.0 / narrowest**2 + 1.0 / north_spacing**2)
    )
    coriolis = TURN_RATE * jnp.sin(latitude) / time_step
    turning = coriolis * (STEPS * time_step)
    return (cosine, east_spacing, north_spacing, time_step, coriolis, turning)


def north_diff(values):
    padded = jnp.pad(values, ((0, 0), (1, 1)))
    return padded[:, 2:] - padded[:, :-2]


def advance_split(state, depth, consts):
    cosine, east_spacing, north_spacing, time_step, coriolis, turning = consts
    height = state[0]
    zonal = state[1]
    merid = state[2]
    flux_wide = padded_2(depth * zonal, (("lon", 0),), 1)
    flux_north = depth * merid * cosine
    diverge = (flux_wide[2:] - flux_wide[:-2]) / (2.0 * east_spacing) + north_diff(flux_north) / (
        2.0 * north_spacing * cosine
    )
    height_new = height - time_step * diverge
    height_wide = padded_2(height_new, (("lon", 0),), 1)
    zonal_new = zonal + time_step * (
        coriolis * merid - GRAVITY * (height_wide[2:] - height_wide[:-2]) / (2.0 * east_spacing)
    )
    merid_new = merid + time_step * (
        -coriolis * zonal_new - GRAVITY * north_diff(height_new) / (2.0 * north_spacing)
    )
    return jnp.stack([height_new, zonal_new, merid_new])


def rotate(state, angle):
    cos_angle = jnp.cos(angle)
    sin_angle = jnp.sin(angle)
    zonal = state[..., 1, :, :]
    merid = state[..., 2, :, :]
    return jnp.stack(
        [
            state[..., 0, :, :],
            zonal * cos_angle + merid * sin_angle,
            merid * cos_angle - zonal * sin_angle,
        ],
        axis=-3,
    )


def body(start, depth):
    lon_cells = start.shape[1] * lax.axis_size("lon")
    lat_cells = start.shape[2]
    consts = grid_constants(lon_cells, lat_cells)
    turning = consts[5]
    number = lax.axis_index("tm").astype(jnp.float32)
    guess = rotate(start, number * turning)
    ends = guess
    for round_index in range(ROUNDS):
        state = guess
        for turn_index in range(STEPS):
            state = advance_split(state, depth, consts)
        correct = state - rotate(guess, turning)
        carried = rotate(correct, -(number + 1.0) * turning)
        stacked = lax.all_to_all(carried[None], "tm", split_axis=2, concat_axis=0, tiled=True)
        running = jnp.cumsum(stacked, axis=0)
        running = jnp.concatenate([jnp.zeros_like(stacked[:1]), running[:-1]], axis=0)
        before = lax.all_to_all(running, "tm", split_axis=0, concat_axis=2, tiled=True)[0]
        total = start + before
        if round_index + 1 < ROUNDS:
            guess = rotate(total, number * turning)
        else:
            ends = rotate(total + carried, (number + 1.0) * turning)
    return ends[None]


def solution(mesh):
    return jax.shard_map(
        body,
        mesh=mesh,
        in_specs=(P(None, "lon", None), P("lon", None)),
        out_specs=P("tm", None, "lon", None),
        check_vma=False,
    )
```

profile of v0, /device:TPU:0, one launch (start us, length us, event | category | flops | bytes accessed | tf_op | source)
XLA Modules:
  0.0 90.6 jit_solution(3166907388512287676)
XLA Ops:
  0.2 1.0 %multiply_multiply_fusion.5 = (f32[32,512]{1,0:T(8,128)S(1)}, f32[32,512]{1,0:T(8,128)S(1)}, f32[32,512]{1,0:T(8,128)S(1)}) fusion(f32[32,512]{1,0:T(8,128)} %param.3, f32[512]{0:T(512)S(1)} %fusion.117, f32[512]{0:T(512)S(1)} %get-tuple-element.70, f32[3,32,512]{2,1,0:T(8,128)} %param.2, f32[512]{0:T(512)S(1)} %get-tuple-element.71), kind=kLoop, calls=%fused_computation.196 | loop fusion | flops 147456 | bytes 399360 | tf_op jit(solution)/shard_map/mul | solution.py:62
  1.1 2.5 %collective-permute-start = (f32[1,512]{1,0:T(1,128)S(1)}, f32[1,512]{1,0:T(1,128)S(1)}, u32[]{:S(2)}, u32[]{:S(2)}) collective-permute-start(f32[1,512]{1,0:T(1,128)S(1)} %get-tuple-element.68), channel_id=1, source_target_pairs={{1,0},{2,1},{3,2},{0,3},{5,4},{6,5},{7,6},{4,7},{9,8},{10,9},{11,1... | collective-permute-start | bytes 6152 | tf_op jit(solution)/shard_map/ppermute | solution.py:28
  3.8 1.1 %collective-permute-done = f32[1,512]{1,0:T(1,128)S(1)} collective-permute-done((f32[1,512]{1,0:T(1,128)S(1)}, f32[1,512]{1,0:T(1,128)S(1)}, u32[]{:S(2)}, u32[]{:S(2)}) %collective-permute-start) | collective-permute-done | bytes 2080 | tf_op jit(solution)/shard_map/ppermute | solution.py:28
  4.9 1.7 %collective-permute-done.1 = f32[1,512]{1,0:T(1,128)S(1)} collective-permute-done((f32[1,512]{1,0:T(1,128)S(1)}, f32[1,512]{1,0:T(1,128)S(1)}, u32[]{:S(2)}, u32[]{:S(2)}) %collective-permute-start.1) | collective-permute-done | bytes 2080 | tf_op jit(solution)/shard_map/ppermute | solution.py:26
  7.4 0.8 collective-permute-done.2
  8.1 1.8 %collective-permute-done.3 = f32[1,512]{1,0:T(1,128)S(1)} collective-permute-done((f32[1,512]{1,0:T(1,128)S(1)}, f32[1,512]{1,0:T(1,128)S(1)}, u32[]{:S(2)}, u32[]{:S(2)}) %collective-permute-start.3) | collective-permute-done | bytes 2080 | tf_op jit(solution)/shard_map/ppermute | solution.py:26
  10.6 0.7 collective-permute-done.4
  11.3 1.8 %collective-permute-done.5 = f32[1,512]{1,0:T(1,128)S(1)} collective-permute-done((f32[1,512]{1,0:T(1,128)S(1)}, f32[1,512]{1,0:T(1,128)S(1)}, u32[]{:S(2)}, u32[]{:S(2)}) %collective-permute-start.5) | collective-permute-done | bytes 2080 | tf_op jit(solution)/shard_map/ppermute | solution.py:26
  13.8 0.8 collective-permute-done.6
  14.6 1.8 %collective-permute-done.7 = f32[1,512]{1,0:T(1,128)S(1)} collective-permute-done((f32[1,512]{1,0:T(1,128)S(1)}, f32[1,512]{1,0:T(1,128)S(1)}, u32[]{:S(2)}, u32[]{:S(2)}) %collective-permute-start.7) | collective-permute-done | bytes 2080 | tf_op jit(solution)/shard_map/ppermute | solution.py:26
  17.1 0.7 collective-permute-done.8
  17.8 1.8 %collective-permute-done.9 = f32[1,512]{1,0:T(1,128)S(1)} collective-permute-done((f32[1,512]{1,0:T(1,128)S(1)}, f32[1,512]{1,0:T(1,128)S(1)}, u32[]{:S(2)}, u32[]{:S(2)}) %collective-permute-start.9) | collective-permute-done | bytes 2080 | tf_op jit(solution)/shard_map/ppermute | solution.py:26
  20.3 0.7 collective-permute-done.10
  21.0 1.8 %collective-permute-done.11 = f32[1,512]{1,0:T(1,128)S(1)} collective-permute-done((f32[1,512]{1,0:T(1,128)S(1)}, f32[1,512]{1,0:T(1,128)S(1)}, u32[]{:S(2)}, u32[]{:S(2)}) %collective-permute-start.11) | collective-permute-done | bytes 2080 | tf_op jit(solution)/shard_map/ppermute | solution.py:26
  23.2 13.4 %all_to_all.66 = f32[1,3,32,512]{3,0,1,2:T(1,128)S(1)} all-to-all(f32[1,3,32,512]{3,0,1,2:T(1,128)S(1)} %copy.63), channel_id=1, replica_groups=mesh['tm'=8,'lon'=4] {'tm'}, dimensions={2} | all-to-all | bytes 393216 | tf_op jit(solution)/shard_map/all_to_all | solution.py:106
  36.8 10.2 %all_to_all.67 = f32[8,3,4,512]{3,2,1,0:T(4,128)S(1)} all-to-all(f32[8,3,4,512]{3,2,1,0:T(4,128)S(1)} %concatenate.102.clone), channel_id=1, replica_groups=mesh['tm'=8,'lon'=4] {'tm'}, dimensions={0} | all-to-all | bytes 393216 | tf_op jit(solution)/shard_map/all_to_all | solution.py:109
  47.7 0.8 collective-permute-done.12
  48.5 1.8 %collective-permute-done.13 = f32[1,512]{1,0:T(1,128)S(1)} collective-permute-done((f32[1,512]{1,0:T(1,128)S(1)}, f32[1,512]{1,0:T(1,128)S(1)}, u32[]{:S(2)}, u32[]{:S(2)}) %collective-permute-start.13) | collective-permute-done | bytes 2080 | tf_op jit(solution)/shard_map/ppermute | solution.py:26
  51.0 0.8 collective-permute-done.14
  51.8 1.8 %collective-permute-done.15 = f32[1,512]{1,0:T(1,128)S(1)} collective-permute-done((f32[1,512]{1,0:T(1,128)S(1)}, f32[1,512]{1,0:T(1,128)S(1)}, u32[]{:S(2)}, u32[]{:S(2)}) %collective-permute-start.15) | collective-permute-done | bytes 2080 | tf_op jit(solution)/shard_map/ppermute | solution.py:26
  54.3 0.7 collective-permute-done.16
  55.0 1.8 %collective-permute-done.17 = f32[1,512]{1,0:T(1,128)S(1)} collective-permute-done((f32[1,512]{1,0:T(1,128)S(1)}, f32[1,512]{1,0:T(1,128)S(1)}, u32[]{:S(2)}, u32[]{:S(2)}) %collective-permute-start.17) | collective-permute-done | bytes 2080 | tf_op jit(solution)/shard_map/ppermute | solution.py:26
  57.4 0.8 collective-permute-done.18
  58.2 1.8 %collective-permute-done.19 = f32[1,512]{1,0:T(1,128)S(1)} collective-permute-done((f32[1,512]{1,0:T(1,128)S(1)}, f32[1,512]{1,0:T(1,128)S(1)}, u32[]{:S(2)}, u32[]{:S(2)}) %collective-permute-start.19) | collective-permute-done | bytes 2080 | tf_op jit(solution)/shard_map/ppermute | solution.py:26
  60.7 0.7 collective-permute-done.20
  61.4 1.8 %collective-permute-done.21 = f32[1,512]{1,0:T(1,128)S(1)} collective-permute-done((f32[1,512]{1,0:T(1,128)S(1)}, f32[1,512]{1,0:T(1,128)S(1)}, u32[]{:S(2)}, u32[]{:S(2)}) %collective-permute-start.21) | collective-permute-done | bytes 2080 | tf_op jit(solution)/shard_map/ppermute | solution.py:26
  63.9 0.8 collective-permute-done.22
  64.7 1.8 %collective-permute-done.23 = f32[1,512]{1,0:T(1,128)S(1)} collective-permute-done((f32[1,512]{1,0:T(1,128)S(1)}, f32[1,512]{1,0:T(1,128)S(1)}, u32[]{:S(2)}, u32[]{:S(2)}) %collective-permute-start.23) | collective-permute-done | bytes 2080 | tf_op jit(solution)/shard_map/ppermute | solution.py:26
  66.8 10.9 %all_to_all.68 = f32[1,3,32,512]{3,0,1,2:T(1,128)S(1)} all-to-all(f32[1,3,32,512]{3,0,1,2:T(1,128)S(1)} %copy.67), channel_id=1, replica_groups=mesh['tm'=8,'lon'=4] {'tm'}, dimensions={2} | all-to-all | bytes 393216 | tf_op jit(solution)/shard_map/all_to_all | solution.py:106
  77.9 0.7 concatenate.115.clone
  78.6 3.4 %all-to-all-start.3 = ((f32[8,3,4,512]{3,2,1,0:T(4,128)}), f32[8,3,4,512]{3,2,1,0:T(4,128)S(1)}, u32[]{:S(2)}, u32[]{:S(2)}) async-start(f32[8,3,4,512]{3,2,1,0:T(4,128)} %concatenate.115.clone), calls=%async_computation.3 | async-start | bytes 393216 | tf_op jit(solution)/shard_map/all_to_all | solution.py:109
  82.1 7.6 %all-to-all-done.3 = f32[8,3,4,512]{3,2,1,0:T(4,128)S(1)} async-done(((f32[8,3,4,512]{3,2,1,0:T(4,128)}), f32[8,3,4,512]{3,2,1,0:T(4,128)S(1)}, u32[]{:S(2)}, u32[]{:S(2)}) %all-to-all-start.3) | async-done | bytes 196640 | tf_op jit(solution)/shard_map/all_to_all | solution.py:109
  (91 shorter events, 10.0 us)
Async XLA Ops:
  0.1 6.5 %copy-start.1 = (f32[3,32,512]{2,1,0:T(8,128)S(1)}, f32[3,32,512]{2,1,0:T(8,128)}, u32[]{:S(2)}) copy-start(f32[3,32,512]{2,1,0:T(8,128)} %param.2) | copy-start | bytes 589828
  1.1 3.8 %collective-permute-start = (f32[1,512]{1,0:T(1,128)S(1)}, f32[1,512]{1,0:T(1,128)S(1)}, u32[]{:S(2)}, u32[]{:S(2)}) collective-permute-start(f32[1,512]{1,0:T(1,128)S(1)} %get-tuple-element.68), channel_id=1, source_target_pairs={{1,0},{2,1},{3,2},{0,3},{5,4},{6,5},{7,6},{4,7},{9,8},{10,9},{11,1... | collective-permute-start | bytes 6152 | tf_op jit(solution)/shard_map/ppermute | solution.py:28
  3.6 3.0 %collective-permute-start.1 = (f32[1,512]{1,0:T(1,128)S(1)}, f32[1,512]{1,0:T(1,128)S(1)}, u32[]{:S(2)}, u32[]{:S(2)}) collective-permute-start(f32[1,512]{1,0:T(1,128)S(1)} %get-tuple-element.69), channel_id=1, source_target_pairs={{0,1},{1,2},{2,3},{3,0},{4,5},{5,6},{6,7},{7,4},{8,9},{9,10},{10,1... | collective-permute-start | bytes 6152 | tf_op jit(solution)/shard_map/ppermute | solution.py:26
  6.6 3.3 %copy-start = (f32[32,512]{1,0:T(8,128)S(1)}, f32[32,512]{1,0:T(8,128)}, u32[]{:S(2)}) copy-start(f32[32,512]{1,0:T(8,128)} %param.3) | copy-start | bytes 196612
  6.8 1.4 %collective-permute-start.2 = (f32[1,512]{1,0:T(1,128)S(1)}, f32[1,512]{1,0:T(1,128)S(1)}, u32[]{:S(2)}, u32[]{:S(2)}) collective-permute-start(f32[1,512]{1,0:T(1,128)S(1)} %get-tuple-element.66), channel_id=1, source_target_pairs={{1,0},{2,1},{3,2},{0,3},{5,4},{6,5},{7,6},{4,7},{9,8},{10,9},{11,1... | collective-permute-start | bytes 6152 | tf_op jit(solution)/shard_map/ppermute | solution.py:28
  6.8 3.1 %collective-permute-start.3 = (f32[1,512]{1,0:T(1,128)S(1)}, f32[1,512]{1,0:T(1,128)S(1)}, u32[]{:S(2)}, u32[]{:S(2)}) collective-permute-start(f32[1,512]{1,0:T(1,128)S(1)} %get-tuple-element.67), channel_id=1, source_target_pairs={{0,1},{1,2},{2,3},{3,0},{4,5},{5,6},{6,7},{7,4},{8,9},{9,10},{10,1... | collective-permute-start | bytes 6152 | tf_op jit(solution)/shard_map/ppermute | solution.py:26
  10.0 1.4 %collective-permute-start.4 = (f32[1,512]{1,0:T(1,128)S(1)}, f32[1,512]{1,0:T(1,128)S(1)}, u32[]{:S(2)}, u32[]{:S(2)}) collective-permute-start(f32[1,512]{1,0:T(1,128)S(1)} %get-tuple-element.64), channel_id=1, source_target_pairs={{1,0},{2,1},{3,2},{0,3},{5,4},{6,5},{7,6},{4,7},{9,8},{10,9},{11,1... | collective-permute-start | bytes 6152 | tf_op jit(solution)/shard_map/ppermute | solution.py:28
  10.0 3.1 %collective-permute-start.5 = (f32[1,512]{1,0:T(1,128)S(1)}, f32[1,512]{1,0:T(1,128)S(1)}, u32[]{:S(2)}, u32[]{:S(2)}) collective-permute-start(f32[1,512]{1,0:T(1,128)S(1)} %get-tuple-element.65), channel_id=1, source_target_pairs={{0,1},{1,2},{2,3},{3,0},{4,5},{5,6},{6,7},{7,4},{8,9},{9,10},{10,1... | collective-permute-start | bytes 6152 | tf_op jit(solution)/shard_map/ppermute | solution.py:26
  13.2 1.4 %collective-permute-start.6 = (f32[1,512]{1,0:T(1,128)S(1)}, f32[1,512]{1,0:T(1,128)S(1)}, u32[]{:S(2)}, u32[]{:S(2)}) collective-permute-start(f32[1,512]{1,0:T(1,128)S(1)} %get-tuple-element.62), channel_id=1, source_target_pairs={{1,0},{2,1},{3,2},{0,3},{5,4},{6,5},{7,6},{4,7},{9,8},{10,9},{11,1... | collective-permute-start | bytes 6152 | tf_op jit(solution)/shard_map/ppermute | solution.py:28
  13.3 3.1 %collective-permute-start.7 = (f32[1,512]{1,0:T(1,128)S(1)}, f32[1,512]{1,0:T(1,128)S(1)}, u32[]{:S(2)}, u32[]{:S(2)}) collective-permute-start(f32[1,512]{1,0:T(1,128)S(1)} %get-tuple-element.63), channel_id=1, source_target_pairs={{0,1},{1,2},{2,3},{3,0},{4,5},{5,6},{6,7},{7,4},{8,9},{9,10},{10,1... | collective-permute-start | bytes 6152 | tf_op jit(solution)/shard_map/ppermute | solution.py:26
  16.4 1.4 %collective-permute-start.8 = (f32[1,512]{1,0:T(1,128)S(1)}, f32[1,512]{1,0:T(1,128)S(1)}, u32[]{:S(2)}, u32[]{:S(2)}) collective-permute-start(f32[1,512]{1,0:T(1,128)S(1)} %get-tuple-element.60), channel_id=1, source_target_pairs={{1,0},{2,1},{3,2},{0,3},{5,4},{6,5},{7,6},{4,7},{9,8},{10,9},{11,1... | collective-permute-start | bytes 6152 | tf_op jit(solution)/shard_map/ppermute | solution.py:28
  16.5 3.1 %collective-permute-start.9 = (f32[1,512]{1,0:T(1,128)S(1)}, f32[1,512]{1,0:T(1,128)S(1)}, u32[]{:S(2)}, u32[]{:S(2)}) collective-permute-start(f32[1,512]{1,0:T(1,128)S(1)} %get-tuple-element.61), channel_id=1, source_target_pairs={{0,1},{1,2},{2,3},{3,0},{4,5},{5,6},{6,7},{7,4},{8,9},{9,10},{10,1... | collective-permute-start | bytes 6152 | tf_op jit(solution)/shard_map/ppermute | solution.py:26
  19.7 1.4 %collective-permute-start.10 = (f32[1,512]{1,0:T(1,128)S(1)}, f32[1,512]{1,0:T(1,128)S(1)}, u32[]{:S(2)}, u32[]{:S(2)}) collective-permute-start(f32[1,512]{1,0:T(1,128)S(1)} %get-tuple-element.58), channel_id=1, source_target_pairs={{1,0},{2,1},{3,2},{0,3},{5,4},{6,5},{7,6},{4,7},{9,8},{10,9},{11,1... | collective-permute-start | bytes 6152 | tf_op jit(solution)/shard_map/ppermute | solution.py:28
  19.7 3.1 %collective-permute-start.11 = (f32[1,512]{1,0:T(1,128)S(1)}, f32[1,512]{1,0:T(1,128)S(1)}, u32[]{:S(2)}, u32[]{:S(2)}) collective-permute-start(f32[1,512]{1,0:T(1,128)S(1)} %get-tuple-element.59), channel_id=1, source_target_pairs={{0,1},{1,2},{2,3},{3,0},{4,5},{5,6},{6,7},{7,4},{8,9},{9,10},{10,1... | collective-permute-start | bytes 6152 | tf_op jit(solution)/shard_map/ppermute | solution.py:26
  47.2 1.4 %collective-permute-start.12 = (f32[1,512]{1,0:T(1,128)S(1)}, f32[1,512]{1,0:T(1,128)S(1)}, u32[]{:S(2)}, u32[]{:S(2)}) collective-permute-start(f32[1,512]{1,0:T(1,128)S(1)} %get-tuple-element.56), channel_id=1, source_target_pairs={{1,0},{2,1},{3,2},{0,3},{5,4},{6,5},{7,6},{4,7},{9,8},{10,9},{11,1... | collective-permute-start | bytes 6152 | tf_op jit(solution)/shard_map/ppermute | solution.py:28
  47.2 3.1 %collective-permute-start.13 = (f32[1,512]{1,0:T(1,128)S(1)}, f32[1,512]{1,0:T(1,128)S(1)}, u32[]{:S(2)}, u32[]{:S(2)}) collective-permute-start(f32[1,512]{1,0:T(1,128)S(1)} %get-tuple-element.57), channel_id=1, source_target_pairs={{0,1},{1,2},{2,3},{3,0},{4,5},{5,6},{6,7},{7,4},{8,9},{9,10},{10,1... | collective-permute-start | bytes 6152 | tf_op jit(solution)/shard_map/ppermute | solution.py:26
  50.4 1.4 %collective-permute-start.14 = (f32[1,512]{1,0:T(1,128)S(1)}, f32[1,512]{1,0:T(1,128)S(1)}, u32[]{:S(2)}, u32[]{:S(2)}) collective-permute-start(f32[1,512]{1,0:T(1,128)S(1)} %get-tuple-element.54), channel_id=1, source_target_pairs={{1,0},{2,1},{3,2},{0,3},{5,4},{6,5},{7,6},{4,7},{9,8},{10,9},{11,1... | collective-permute-start | bytes 6152 | tf_op jit(solution)/shard_map/ppermute | solution.py:28
  50.5 3.1 %collective-permute-start.15 = (f32[1,512]{1,0:T(1,128)S(1)}, f32[1,512]{1,0:T(1,128)S(1)}, u32[]{:S(2)}, u32[]{:S(2)}) collective-permute-start(f32[1,512]{1,0:T(1,128)S(1)} %get-tuple-element.55), channel_id=1, source_target_pairs={{0,1},{1,2},{2,3},{3,0},{4,5},{5,6},{6,7},{7,4},{8,9},{9,10},{10,1... | collective-permute-start | bytes 6152 | tf_op jit(solution)/shard_map/ppermute | solution.py:26
  53.6 1.4 %collective-permute-start.16 = (f32[1,512]{1,0:T(1,128)S(1)}, f32[1,512]{1,0:T(1,128)S(1)}, u32[]{:S(2)}, u32[]{:S(2)}) collective-permute-start(f32[1,512]{1,0:T(1,128)S(1)} %get-tuple-element.52), channel_id=1, source_target_pairs={{1,0},{2,1},{3,2},{0,3},{5,4},{6,5},{7,6},{4,7},{9,8},{10,9},{11,1... | collective-permute-start | bytes 6152 | tf_op jit(solution)/shard_map/ppermute | solution.py:28
  53.7 3.1 %collective-permute-start.17 = (f32[1,512]{1,0:T(1,128)S(1)}, f32[1,512]{1,0:T(1,128)S(1)}, u32[]{:S(2)}, u32[]{:S(2)}) collective-permute-start(f32[1,512]{1,0:T(1,128)S(1)} %get-tuple-element.53), channel_id=1, source_target_pairs={{0,1},{1,2},{2,3},{3,0},{4,5},{5,6},{6,7},{7,4},{8,9},{9,10},{10,1... | collective-permute-start | bytes 6152 | tf_op jit(solution)/shard_map/ppermute | solution.py:26
  56.9 1.4 %collective-permute-start.18 = (f32[1,512]{1,0:T(1,128)S(1)}, f32[1,512]{1,0:T(1,128)S(1)}, u32[]{:S(2)}, u32[]{:S(2)}) collective-permute-start(f32[1,512]{1,0:T(1,128)S(1)} %get-tuple-element.50), channel_id=1, source_target_pairs={{1,0},{2,1},{3,2},{0,3},{5,4},{6,5},{7,6},{4,7},{9,8},{10,9},{11,1... | collective-permute-start | bytes 6152 | tf_op jit(solution)/shard_map/ppermute | solution.py:28
  56.9 3.1 %collective-permute-start.19 = (f32[1,512]{1,0:T(1,128)S(1)}, f32[1,512]{1,0:T(1,128)S(1)}, u32[]{:S(2)}, u32[]{:S(2)}) collective-permute-start(f32[1,512]{1,0:T(1,128)S(1)} %get-tuple-element.51), channel_id=1, source_target_pairs={{0,1},{1,2},{2,3},{3,0},{4,5},{5,6},{6,7},{7,4},{8,9},{9,10},{10,1... | collective-permute-start | bytes 6152 | tf_op jit(solution)/shard_map/ppermute | solution.py:26
  60.0 1.4 %collective-permute-start.20 = (f32[1,512]{1,0:T(1,128)S(1)}, f32[1,512]{1,0:T(1,128)S(1)}, u32[]{:S(2)}, u32[]{:S(2)}) collective-permute-start(f32[1,512]{1,0:T(1,128)S(1)} %get-tuple-element.48), channel_id=1, source_target_pairs={{1,0},{2,1},{3,2},{0,3},{5,4},{6,5},{7,6},{4,7},{9,8},{10,9},{11,1... | collective-permute-start | bytes 6152 | tf_op jit(solution)/shard_map/ppermute | solution.py:28
  60.1 3.1 %collective-permute-start.21 = (f32[1,512]{1,0:T(1,128)S(1)}, f32[1,512]{1,0:T(1,128)S(1)}, u32[]{:S(2)}, u32[]{:S(2)}) collective-permute-start(f32[1,512]{1,0:T(1,128)S(1)} %get-tuple-element.49), channel_id=1, source_target_pairs={{0,1},{1,2},{2,3},{3,0},{4,5},{5,6},{6,7},{7,4},{8,9},{9,10},{10,1... | collective-permute-start | bytes 6152 | tf_op jit(solution)/shard_map/ppermute | solution.py:26
  63.3 1.4 %collective-permute-start.22 = (f32[1,512]{1,0:T(1,128)S(1)}, f32[1,512]{1,0:T(1,128)S(1)}, u32[]{:S(2)}, u32[]{:S(2)}) collective-permute-start(f32[1,512]{1,0:T(1,128)S(1)} %get-tuple-element.46), channel_id=1, source_target_pairs={{1,0},{2,1},{3,2},{0,3},{5,4},{6,5},{7,6},{4,7},{9,8},{10,9},{11,1... | collective-permute-start | bytes 6152 | tf_op jit(solution)/shard_map/ppermute | solution.py:28
  63.4 3.1 %collective-permute-start.23 = (f32[1,512]{1,0:T(1,128)S(1)}, f32[1,512]{1,0:T(1,128)S(1)}, u32[]{:S(2)}, u32[]{:S(2)}) collective-permute-start(f32[1,512]{1,0:T(1,128)S(1)} %get-tuple-element.47), channel_id=1, source_target_pairs={{0,1},{1,2},{2,3},{3,0},{4,5},{5,6},{6,7},{7,4},{8,9},{9,10},{10,1... | collective-permute-start | bytes 6152 | tf_op jit(solution)/shard_map/ppermute | solution.py:26
  78.6 11.1 %all-to-all-start.3 = ((f32[8,3,4,512]{3,2,1,0:T(4,128)}), f32[8,3,4,512]{3,2,1,0:T(4,128)S(1)}, u32[]{:S(2)}, u32[]{:S(2)}) async-start(f32[8,3,4,512]{3,2,1,0:T(4,128)} %concatenate.115.clone), calls=%async_computation.3 | async-start | bytes 393216 | tf_op jit(solution)/shard_map/all_to_all | solution.py:109
where the time goes:
time: 90.9 us; the launch traced here: 90.6 us
  waiting for transfers between devices  38 us (42%)
  blocking collectives  34.5 us (38%)
  starting transfers between devices  12 us (13%)
  other arithmetic  4.07 us (4%)
  local copies, waits for them, and re-layouts  1.53 us (2%)
    all_to_all x2, blocking collectives, body(): lax.all_to_all(carried[None], 'tm', split_axis=2, concat_axis=0, tiled=True)  24.3 us
    ppermute x12, waiting for transfers between devices, padded_2(): lax.ppermute(tail, axis, [(i, (i + 1) % count) for i in range(count)])  21.1 us
    all_to_all x1, blocking collectives, body(): lax.all_to_all(running, 'tm', split_axis=0, concat_axis=2, tiled=True)[0]  10.2 us
    ppermute x12, waiting for transfers between devices, padded_2(): lax.ppermute(head, axis, [((i + 1) % count, i) for i in range(count)])  9.29 us
    all_to_all x1, waiting for transfers between devices, body(): lax.all_to_all(running, 'tm', split_axis=0, concat_axis=2, tiled=True)[0]  7.62 us
    ppermute x12, starting transfers between devices, padded_2(): lax.ppermute(tail, axis, [(i, (i + 1) % count) for i in range(count)])  5.47 us
    all_to_all x1, starting transfers between devices, body(): lax.all_to_all(running, 'tm', split_axis=0, concat_axis=2, tiled=True)[0]  3.39 us
    ppermute x12, starting transfers between devices, padded_2(): lax.ppermute(head, axis, [((i + 1) % count, i) for i in range(count)])  3.12 us
  transfers between devices with their start and end apart: 25, of which 25 were waited for; matrix products, arithmetic and copies ran while one was open for 1% of the time, Pallas kernels for 0%

commit v1 on v0

v1 whole, which is shorter than its diff:
```python
import math

import jax
import jax.numpy as jnp
import numpy as np
from jax import lax
from jax.experimental import pallas as pl
from jax.experimental.pallas import tpu as pltpu
from jax.sharding import PartitionSpec as P

STEPS = 3
ROUNDS = 2
LAT_LIMIT = 1.2
COURANT = 1.2
DEPTH_MAX = 1.5
GRAVITY = 1.0
TURN_RATE = 0.15

HALO = 2 * STEPS * ROUNDS
ROWS = 8
LANES = 128
VMEM_LIMIT = 16 << 20

EAST, POLE, DIVERGE, SPIN_U, SPIN_V, GRAD_E, GRAD_N, TURN_C, TURN_U, TURN_V, EAST_INV, POLE_INV = range(12)


def lat_table(lon_cells, lat_cells):
    latitude = -LAT_LIMIT + (np.arange(lat_cells) + 0.5) * (2.0 * LAT_LIMIT / lat_cells)
    cosine = np.cos(latitude)
    north_spacing = 2.0 * LAT_LIMIT / lat_cells
    east_spacing = cosine * (2.0 * math.pi / lon_cells)
    narrowest = math.cos(LAT_LIMIT - LAT_LIMIT / lat_cells) * 2.0 * math.pi / lon_cells
    time_step = COURANT / (
        math.sqrt(DEPTH_MAX * GRAVITY) * math.sqrt(1.0 / narrowest**2 + 1.0 / north_spacing**2)
    )
    spin = TURN_RATE * np.sin(latitude)
    turning = spin * STEPS
    east = time_step / (2.0 * east_spacing)
    north = time_step / (2.0 * north_spacing)
    rows = [None] * 12
    rows[EAST] = east
    rows[POLE] = cosine
    rows[DIVERGE] = north / cosine
    rows[SPIN_U] = spin * east / cosine
    rows[SPIN_V] = spin * cosine / east
    rows[GRAD_E] = GRAVITY * east
    rows[GRAD_N] = GRAVITY * north + 0.0 * cosine
    rows[TURN_C] = np.cos(turning)
    rows[TURN_U] = np.sin(turning) * east / cosine
    rows[TURN_V] = np.sin(turning) * cosine / east
    rows[EAST_INV] = 1.0 / east
    rows[POLE_INV] = 1.0 / cosine
    table = np.stack(rows).astype(np.float32)
    return np.broadcast_to(table[:, None, :], (12, ROWS, lat_cells)).copy()


def windows(low, high):
    starts = list(range(low, high - ROWS + 1, ROWS))
    if starts[-1] + ROWS < high:
        starts.append(high - ROWS)
    return starts


def kernel(cells, tiles, start, depth, left, right, table, ends, *scratch):
    (s_h, u_a, u_b, v_h, v_a, v_b, w_h, w_a, w_b, grad_e, grad_n, inverse) = scratch[:12]
    temps1 = scratch[12:18]
    temps2 = scratch[18:24]
    wide = cells + 2 * HALO
    number = lax.axis_index("tm")
    lane = lax.broadcasted_iota(jnp.int32, (ROWS, LANES), 1)
    first = lane == 0
    last = lane == LANES - 1
    zero = jnp.zeros((ROWS, LANES), jnp.float32)

    def const(row, t):
        return table[row, :, t * LANES : (t + 1) * LANES]

    def at(ref, t, row):
        return ref[t, row : row + ROWS, :]

    def put(ref, t, row, value):
        ref[t, row : row + ROWS, :] = value

    def north_diff(parts):
        out = []
        for t in range(tiles):
            above = parts[t + 1] if t + 1 < tiles else zero
            below = parts[t - 1] if t > 0 else zero
            up = pltpu.roll(jnp.where(first, above, parts[t]), LANES - 1, 1)
            down = pltpu.roll(jnp.where(last, below, parts[t]), 1, 1)
            out.append(up - down)
        return out

    def load_block(field_of, depth_of, count, base):
        for row in windows(0, count):
            for t in range(tiles):
                h = depth_of(row, t)
                he = h * const(EAST, t)
                hp = h * const(POLE, t)
                put(s_h, t, base + row, field_of(0, row, t))
                put(u_a, t, base + row, field_of(1, row, t) * he)
                put(u_b, t, base + row, field_of(2, row, t) * hp)
                put(grad_e, t, base + row, he * const(GRAD_E, t))
                put(grad_n, t, base + row, hp * const(GRAD_N, t))

    def part(ref, *lead):
        return lambda row, t: ref[(*lead, slice(row, row + ROWS), slice(t * LANES, (t + 1) * LANES))]

    load_block(lambda f, r, t: part(start, f)(r, t), part(depth), cells, HALO)
    load_block(lambda f, r, t: part(left, f)(r, t), part(left, 3), HALO, 0)
    load_block(lambda f, r, t: part(right, f)(r, t), part(right, 3), HALO, HALO + cells)

    def fine(source, low, high, temps):
        state = source
        for step in range(STEPS):
            height, alpha, beta = state
            new = temps[3 * (step % 2) : 3 * (step % 2) + 3]
            new_h, new_a, new_b = new
            for row in windows(low + 1, high - 1):
                flux = north_diff([at(beta, t, row) for t in range(tiles)])
                for t in range(tiles):
                    value = at(height, t, row) - (at(alpha, t, row + 1) - at(alpha, t, row - 1))
                    put(new_h, t, row, value - const(DIVERGE, t) * flux[t])
            for row in windows(low + 2, high - 2):
                slope = north_diff([at(new_h, t, row) for t in range(tiles)])
                for t in range(tiles):
                    b = at(beta, t, row)
                    east = at(new_h, t, row + 1) - at(new_h, t, row - 1)
                    a = at(alpha, t, row) + const(SPIN_U, t) * b - at(grad_e, t, row) * east
                    put(new_a, t, row, a)
                    b = b - const(SPIN_V, t) * a - at(grad_n, t, row) * slope[t]
                    put(new_b, t, row, b)
            state = new
            low, high = low + 2, high - 2
        return state

    def turn(a, b, t):
        c = const(TURN_C, t)
        return c * a + const(TURN_U, t) * b, c * b - const(TURN_V, t) * a

    reach = 2 * STEPS

    def round_one(first_time):
        x_h, x_a, x_b = fine((s_h, u_a, u_b), 0, wide, temps1)
        for row in windows(reach, wide - reach):
            for t in range(tiles):
                xh, xa, xb = at(x_h, t, row), at(x_a, t, row), at(x_b, t, row)
                if not first_time:
                    xh = xh + (at(v_h, t, row) - at(s_h, t, row))
                    a, b = turn(
                        at(v_a, t, row) - at(u_a, t, row), at(v_b, t, row) - at(u_b, t, row), t
                    )
                    xa, xb = xa + a, xb + b
                put(n_h, t, row, xh)
                put(n_a, t, row, xa)
                put(n_b, t, row, xb)

    n_h, n_a, n_b = scratch[24:27]

    def turn_guess():
        for row in range(0, wide, ROWS):
            for t in range(tiles):
                a, b = turn(at(u_a, t, row), at(u_b, t, row), t)
                put(u_a, t, row, a)
                put(u_b, t, row, b)

    def move(low, high, targets):
        for row in windows(low, high):
            for t in range(tiles):
                for source, target in zip((n_h, n_a, n_b), targets):
                    put(target, t, row, at(source, t, row))

    def round_two():
        y = fine((v_h, v_a, v_b), reach, wide - reach, temps2)
        for row in windows(HALO, HALO + cells):
            for t in range(tiles):
                yh, ya, yb = (at(ref, t, row) for ref in y)
                yh = yh + (at(w_h, t, row) - at(v_h, t, row))
                a, b = turn(at(w_a, t, row) - at(v_a, t, row), at(w_b, t, row) - at(v_b, t, row), t)
                put(w_h, t, row, yh)
                put(w_a, t, row, ya + a)
                put(w_b, t, row, yb + b)

    round_one(True)
    move(reach, wide - reach, (v_h, v_a, v_b))
    move(HALO, HALO + cells, (w_h, w_a, w_b))

    def both(index, carry):
        turn_guess()
        round_one(False)
        round_two()
        move(reach, wide - reach, (v_h, v_a, v_b))
        return carry

    lax.fori_loop(1, number, both, 0)

    @pl.when(number > 0)
    def _():
        round_two()

    for row in windows(0, cells):
        for t in range(tiles):
            span = (slice(row, row + ROWS), slice(t * LANES, (t + 1) * LANES))
            over = 1.0 / depth[span]
            ends[(0, 0, *span)] = at(w_h, t, HALO + row)
            ends[(0, 1, *span)] = at(w_a, t, HALO + row) * (over * const(EAST_INV, t))
            ends[(0, 2, *span)] = at(w_b, t, HALO + row) * (over * const(POLE_INV, t))


def body(start, depth):
    count = lax.axis_size("lon")
    _, cells, lat_cells = start.shape
    tiles = lat_cells // LANES
    table = lat_table(cells * count, lat_cells)
    both = jnp.concatenate([start, depth[None]], axis=0)
    left = lax.ppermute(both[:, cells - HALO :], "lon", [(i, (i + 1) % count) for i in range(count)])
    right = lax.ppermute(both[:, :HALO], "lon", [((i + 1) % count, i) for i in range(count)])
    wide = cells + 2 * HALO
    vmem = pl.BlockSpec(memory_space=pltpu.VMEM)

    def run(*refs):
        kernel(cells, tiles, *refs)

    return pl.pallas_call(
        run,
        out_shape=jax.ShapeDtypeStruct((1, *start.shape), jnp.float32),
        in_specs=[vmem] * 5,
        out_specs=vmem,
        scratch_shapes=[pltpu.VMEM((tiles, wide, LANES), jnp.float32)] * 27,
        compiler_params=pltpu.CompilerParams(vmem_limit_bytes=VMEM_LIMIT),
        name="parareal",
    )(start, depth, left, right, jnp.asarray(table))


def solution(mesh):
    return jax.shard_map(
        body,
        mesh=mesh,
        in_specs=(P(None, "lon", None), P("lon", None)),
        out_specs=P("tm", None, "lon", None),
        check_vma=False,
    )
```

time: 90.9 us -> 16.3 us (0.18)
  the two profiles are of different devices: /device:TPU:0 before, /device:TPU:31 now
where the time goes in v1:
time: 16.3 us; the launch traced here: 16.1 us
  Pallas kernels  8.96 us (55%)
  waiting for transfers between devices  4.29 us (26%)
  starting transfers between devices  1.8 us (11%)
  other arithmetic  1.06 us (7%)
    pallas_call x1, Pallas kernels, body(): pl.pallas_call(run, out_shape=jax.ShapeDtypeStruct((1, *start.shape), jnp...  8.96 us
    ppermute x1, waiting for transfers between devices, body(): lax.ppermute(both[:, :HALO], 'lon', [((i + 1) % count, i) for i in range(...  4.29 us
    ppermute x1, starting transfers between devices, body(): lax.ppermute(both[:, cells - HALO:], 'lon', [(i, (i + 1) % count) for i i...  1.07 us
    concatenate x1, other arithmetic, body(): both = jnp.concatenate([start, depth[None]], axis=0)  1.06 us
    ppermute x1, starting transfers between devices, body(): lax.ppermute(both[:, :HALO], 'lon', [((i + 1) % count, i) for i in range(...  0.73 us
  transfers between devices with their start and end apart: 2, of which 1 were waited for; matrix products, arithmetic and copies ran while one was open for 0% of the time, Pallas kernels for 0%

profile of v1, /device:TPU:31, one launch (start us, length us, event | category | flops | bytes accessed | tf_op | source)
XLA Modules:
  0.0 16.1 jit_solution(9651023129503073920)
XLA Ops:
  0.0 0.0 copy-start
  0.0 0.0 copy-start.1
  0.0 0.0 copy-start.2
  0.0 1.1 %pad_maximum_fusion = (f32[4,12,512]{2,1,0:T(8,128)S(1)}, f32[4,12,512]{2,1,0:T(8,128)S(1)}) fusion(f32[1,32,512]{2,1,0:T(8,128)} %bitcast.1, f32[3,32,512]{2,1,0:T(8,128)} %refs_0_.1), kind=kLoop, calls=%fused_computation.3 | loop fusion | flops 49152 | bytes 458752 | tf_op jit(solution)/shard_map/concatenate | solution.py:215
  1.1 0.7 %collective-permute-start.1 = (f32[4,12,512]{2,1,0:T(8,128)S(1)}, f32[4,12,512]{2,1,0:T(8,128)S(1)}, u32[]{:S(2)}, u32[]{:S(2)}) collective-permute-start(f32[4,12,512]{2,1,0:T(8,128)S(1)} %get-tuple-element.5), channel_id=1, source_target_pairs={{1,0},{2,1},{3,2},{0,3},{5,4},{6,5},{7,6},{4,7},{9,8},{10,9},{11,1... | collective-permute-start | bytes 294920 | tf_op jit(solution)/shard_map/ppermute | solution.py:217
  1.8 1.1 %collective-permute-start = (f32[4,12,512]{2,1,0:T(8,128)S(1)}, f32[4,12,512]{2,1,0:T(8,128)S(1)}, u32[]{:S(2)}, u32[]{:S(2)}) collective-permute-start(f32[4,12,512]{2,1,0:T(8,128)S(1)} %get-tuple-element.6), channel_id=1, source_target_pairs={{0,1},{1,2},{2,3},{3,0},{4,5},{5,6},{6,7},{7,4},{8,9},{9,10},{10,1... | collective-permute-start | bytes 294920 | tf_op jit(solution)/shard_map/ppermute | solution.py:216
  2.9 4.3 %collective-permute-done.1.refs_3_ = f32[4,12,512]{2,1,0:T(8,128)S(1)} collective-permute-done((f32[4,12,512]{2,1,0:T(8,128)S(1)}, f32[4,12,512]{2,1,0:T(8,128)S(1)}, u32[]{:S(2)}, u32[]{:S(2)}) %collective-permute-start.1) | collective-permute-done | bytes 98336 | tf_op jit(solution)/shard_map/ppermute | solution.py:217
  7.2 0.0 collective-permute-done.refs_2_
  7.2 0.0 copy-done
  7.2 0.0 copy-done.1
  7.2 0.0 copy-done.2
  7.2 9.0 %parareal.1 = f32[1,3,32,512]{3,2,1,0:T(8,128)} custom-call(f32[3,32,512]{2,1,0:T(8,128)S(1)} %copy-done, f32[32,512]{1,0:T(8,128)S(1)} %copy-done.1, f32[4,12,512]{2,1,0:T(8,128)S(1)} %collective-permute-done.refs_2_, f32[4,12,512]{2,1,0:T(8,128)S(1)} %collective-permute-done.1.refs_3_, f32[12,8,512]{2,1,0:T(8,128)S(1)} %copy-done.2), custom_call_target="tpu_custom_call" | custom-call | tf_op jit(solution)/shard_map/parareal/pallas_call | solution.py:224
Async XLA Ops:
  0.0 7.2 %copy-start = (f32[3,32,512]{2,1,0:T(8,128)S(1)}, f32[3,32,512]{2,1,0:T(8,128)}, u32[]{:S(2)}) copy-start(f32[3,32,512]{2,1,0:T(8,128)} %refs_0_.1) | copy-start | bytes 589828
  0.0 7.2 %copy-start.1 = (f32[32,512]{1,0:T(8,128)S(1)}, f32[32,512]{1,0:T(8,128)}, u32[]{:S(2)}) copy-start(f32[32,512]{1,0:T(8,128)} %refs_1_.1) | copy-start | bytes 196612
  0.0 7.2 %copy-start.2 = (f32[12,8,512]{2,1,0:T(8,128)S(1)}, f32[12,8,512]{2,1,0:T(8,128)}, u32[]{:S(2)}) copy-start(f32[12,8,512]{2,1,0:T(8,128)} %constant.2.clone.refs_4_) | copy-start | bytes 589828
  1.1 6.1 %collective-permute-start.1 = (f32[4,12,512]{2,1,0:T(8,128)S(1)}, f32[4,12,512]{2,1,0:T(8,128)S(1)}, u32[]{:S(2)}, u32[]{:S(2)}) collective-permute-start(f32[4,12,512]{2,1,0:T(8,128)S(1)} %get-tuple-element.5), channel_id=1, source_target_pairs={{1,0},{2,1},{3,2},{0,3},{5,4},{6,5},{7,6},{4,7},{9,8},{10,9},{11,1... | collective-permute-start | bytes 294920 | tf_op jit(solution)/shard_map/ppermute | solution.py:217
  1.8 5.4 %collective-permute-start = (f32[4,12,512]{2,1,0:T(8,128)S(1)}, f32[4,12,512]{2,1,0:T(8,128)S(1)}, u32[]{:S(2)}, u32[]{:S(2)}) collective-permute-start(f32[4,12,512]{2,1,0:T(8,128)S(1)} %get-tuple-element.6), channel_id=1, source_target_pairs={{0,1},{1,2},{2,3},{3,0},{4,5},{5,6},{6,7},{7,4},{8,9},{9,10},{10,1... | collective-permute-start | bytes 294920 | tf_op jit(solution)/shard_map/ppermute | solution.py:216

commit v2 on v1

v2 whole, which is shorter than its diff:
```python
import math

import jax
import jax.numpy as jnp
import numpy as np
from jax import lax
from jax.experimental import pallas as pl
from jax.experimental.pallas import tpu as pltpu
from jax.sharding import PartitionSpec as P

STEPS = 3
ROUNDS = 2
LAT_LIMIT = 1.2
COURANT = 1.2
DEPTH_MAX = 1.5
GRAVITY = 1.0
TURN_RATE = 0.15

HALO = 2 * STEPS * ROUNDS
ROWS = 8
LANES = 128
VMEM_LIMIT = 16 << 20

EAST, POLE, DIVERGE, SPIN_U, SPIN_V, GRAD_E, GRAD_N, TURN_C, TURN_U, TURN_V, EAST_INV, POLE_INV = range(12)


def lat_table(lon_cells, lat_cells):
    latitude = -LAT_LIMIT + (np.arange(lat_cells) + 0.5) * (2.0 * LAT_LIMIT / lat_cells)
    cosine = np.cos(latitude)
    north_spacing = 2.0 * LAT_LIMIT / lat_cells
    east_spacing = cosine * (2.0 * math.pi / lon_cells)
    narrowest = math.cos(LAT_LIMIT - LAT_LIMIT / lat_cells) * 2.0 * math.pi / lon_cells
    time_step = COURANT / (
        math.sqrt(DEPTH_MAX * GRAVITY) * math.sqrt(1.0 / narrowest**2 + 1.0 / north_spacing**2)
    )
    spin = TURN_RATE * np.sin(latitude)
    turning = spin * STEPS
    east = time_step / (2.0 * east_spacing)
    north = time_step / (2.0 * north_spacing)
    rows = [None] * 12
    rows[EAST] = east
    rows[POLE] = cosine
    rows[DIVERGE] = north / cosine
    rows[SPIN_U] = spin * east / cosine
    rows[SPIN_V] = spin * cosine / east
    rows[GRAD_E] = GRAVITY * east
    rows[GRAD_N] = GRAVITY * north + 0.0 * cosine
    rows[TURN_C] = np.cos(turning)
    rows[TURN_U] = np.sin(turning) * east / cosine
    rows[TURN_V] = np.sin(turning) * cosine / east
    rows[EAST_INV] = 1.0 / east
    rows[POLE_INV] = 1.0 / cosine
    table = np.stack(rows).astype(np.float32)
    table = table.reshape(12, LANES, lat_cells // LANES).swapaxes(1, 2).reshape(12, 1, lat_cells)
    return np.broadcast_to(table, (12, ROWS, lat_cells)).copy()


def windows(low, high):
    starts = list(range(low, high - ROWS + 1, ROWS))
    if starts[-1] + ROWS < high:
        starts.append(high - ROWS)
    return starts


def deal(tiles):
    lat = np.arange(tiles * LANES)
    matrix = np.zeros((lat.size, lat.size), np.float32)
    matrix[lat, (lat % tiles) * LANES + lat // tiles] = 1.0
    return matrix


def times_one_hot(values, matrix):
    pieces = []
    rest = values
    for _ in range(3):
        pieces.append(rest.astype(jnp.bfloat16))
        rest = rest - pieces[-1].astype(jnp.float32)
    count = values.shape[0]
    out = jnp.dot(jnp.concatenate(pieces, axis=0), matrix, preferred_element_type=jnp.float32)
    return out[:count] + out[count : 2 * count] + out[2 * count :]


def lanes(t):
    return slice(t * LANES, (t + 1) * LANES)


def put_fields(dealt, table, tiles, count, first_row, step, refs, base):
    for t in range(tiles):
        h, u, v, d = (
            dealt[first_row + f * step : first_row + f * step + count, lanes(t)] for f in range(4)
        )
        he = d * table[EAST, :1, lanes(t)]
        hp = d * table[POLE, :1, lanes(t)]
        rows = slice(base, base + count)
        values = (h, u * he, v * hp, he * table[GRAD_E, :1, lanes(t)], hp * table[GRAD_N, :1, lanes(t)])
        for ref, value in zip(refs, values):
            ref[t, rows, :] = value


def prepare(cells, tiles, start, depth, table, dealing, out):
    own = jnp.concatenate([start[0], start[1], start[2], depth[...]], axis=0)
    dealt = times_one_hot(own, dealing[...])
    put_fields(dealt, table, tiles, cells, 0, cells, [out.at[k] for k in range(5)], 0)
    for t in range(tiles):
        over = 1.0 / dealt[3 * cells :, lanes(t)]
        out[5, t] = over * table[EAST_INV, :1, lanes(t)]
        out[6, t] = over * table[POLE_INV, :1, lanes(t)]


def kernel(cells, tiles, own, left, right, table, dealing, undealing, ends, *scratch):
    (s_h, u_a, u_b, v_h, v_a, v_b, w_h, w_a, w_b, grad_e, grad_n) = scratch[:11]
    temps1 = scratch[11:17]
    temps2 = scratch[17:23]
    wide = cells + 2 * HALO
    reach = 2 * STEPS
    number = lax.axis_index("tm")
    lane = lax.broadcasted_iota(jnp.int32, (ROWS, LANES), 1)
    first = lane == 0
    last = lane == LANES - 1

    def const(row, t):
        return table[row, :, t * LANES : (t + 1) * LANES]

    def at(ref, t, row):
        return ref[t, row : row + ROWS, :]

    def put(ref, t, row, value):
        ref[t, row : row + ROWS, :] = value

    def north_diff(parts):
        above = parts[1:] + [jnp.where(last, 0.0, pltpu.roll(parts[0], LANES - 1, 1))]
        below = [jnp.where(first, 0.0, pltpu.roll(parts[-1], 1, 1))] + parts[:-1]
        return [up - down for up, down in zip(above, below)]

    def consts(*rows):
        return [[const(row, t) for t in range(tiles)] for row in rows]

    fields = (s_h, u_a, u_b, grad_e, grad_n)
    dealt = times_one_hot(jnp.concatenate([left[...], right[...]], axis=0), dealing[...])
    put_fields(dealt, table, tiles, HALO, 0, HALO, fields, 0)
    put_fields(dealt, table, tiles, HALO, 4 * HALO, HALO, fields, HALO + cells)
    for k, ref in enumerate(fields):
        ref[:, HALO : HALO + cells, :] = own[k]

    def fine(source, low, high, temps, finish):
        state = source
        for step in range(STEPS):
            height, alpha, beta = state
            new_h, new_a, new_b = temps[3 * (step % 2) : 3 * (step % 2) + 3]
            (diverge,) = consts(DIVERGE)
            for row in windows(low + 1, high - 1):
                flux = north_diff([at(beta, t, row) for t in range(tiles)])
                for t in range(tiles):
                    value = at(height, t, row) - (at(alpha, t, row + 1) - at(alpha, t, row - 1))
                    put(new_h, t, row, value - diverge[t] * flux[t])
            low, high = low + 2, high - 2
            rows = windows(low, high)
            if step == STEPS - 1:
                rows = list(range(low, high, ROWS))
            spin_u, spin_v = consts(SPIN_U, SPIN_V)
            for row in rows:
                here = [at(new_h, t, row) for t in range(tiles)]
                slope = north_diff(here)
                for t in range(tiles):
                    b = at(beta, t, row)
                    east = at(new_h, t, row + 1) - at(new_h, t, row - 1)
                    a = at(alpha, t, row) + spin_u[t] * b - at(grad_e, t, row) * east
                    b = b - spin_v[t] * a - at(grad_n, t, row) * slope[t]
                    if step == STEPS - 1:
                        finish(t, row, here[t], a, b)
                    else:
                        put(new_a, t, row, a)
                        put(new_b, t, row, b)
            state = (new_h, new_a, new_b)

    def turn(a, b, t):
        c = const(TURN_C, t)
        return c * a + const(TURN_U, t) * b, c * b - const(TURN_V, t) * a

    def first_slice():
        def finish(t, row, h, a, b):
            for ref, value in zip((v_h, v_a, v_b), (h, a, b)):
                put(ref, t, row, value)
            for ref, value in zip((w_h, w_a, w_b), (h, a, b)):
                put(ref, t, row, value)

        fine((s_h, u_a, u_b), 0, wide, temps1, finish)

    def round_one():
        def finish(t, row, h, a, b):
            put(v_h, t, row, h + (at(v_h, t, row) - at(s_h, t, row)))
            da, db = turn(
                at(v_a, t, row) - at(u_a, t, row), at(v_b, t, row) - at(u_b, t, row), t
            )
            put(v_a, t, row, a + da)
            put(v_b, t, row, b + db)

        fine((s_h, u_a, u_b), 0, wide, temps1, finish)

    def turn_guess():
        for row in range(0, wide, ROWS):
            for t in range(tiles):
                a, b = turn(at(u_a, t, row), at(u_b, t, row), t)
                put(u_a, t, row, a)
                put(u_b, t, row, b)

    def round_two():
        def finish(t, row, h, a, b):
            da, db = turn(
                at(w_a, t, row) - at(v_a, t, row), at(w_b, t, row) - at(v_b, t, row), t
            )
            put(w_h, t, row, h + (at(w_h, t, row) - at(v_h, t, row)))
            put(w_a, t, row, a + da)
            put(w_b, t, row, b + db)

        fine((v_h, v_a, v_b), reach, wide - reach, temps2, finish)

    @pl.when(number == 0)
    def _():
        for source, targets in zip((s_h, u_a, u_b), ((v_h, w_h), (v_a, w_a), (v_b, w_b))):
            for target in targets:
                target[...] = source[...]

    pl.when(number > 0)(first_slice)

    def both(index, carry):
        turn_guess()
        round_two()
        round_one()
        return carry

    lax.fori_loop(1, number, both, 0)
    round_two()
    rows = slice(HALO, HALO + cells)
    whole = [
        jnp.concatenate([w_h[t, rows, :] for t in range(tiles)], axis=1),
        jnp.concatenate([w_a[t, rows, :] * own[5, t] for t in range(tiles)], axis=1),
        jnp.concatenate([w_b[t, rows, :] * own[6, t] for t in range(tiles)], axis=1),
    ]
    whole = times_one_hot(jnp.concatenate(whole, axis=0), undealing[...])
    for field in range(3):
        ends[0, field] = whole[field * cells : (field + 1) * cells]


def body(start, depth):
    count = lax.axis_size("lon")
    _, cells, lat_cells = start.shape
    tiles = lat_cells // LANES
    table = lat_table(cells * count, lat_cells)
    dealing = deal(tiles)

    def edge(low, high):
        return jnp.concatenate([start[:, low:high], depth[None, low:high]], axis=0).reshape(-1, lat_cells)

    ring = [(i, (i + 1) % count) for i in range(count)]
    left = lax.ppermute(edge(cells - HALO, cells), "lon", ring)
    right = lax.ppermute(edge(0, HALO), "lon", [(j, i) for i, j in ring])
    wide = cells + 2 * HALO
    vmem = pl.BlockSpec(memory_space=pltpu.VMEM)
    params = pltpu.CompilerParams(vmem_limit_bytes=VMEM_LIMIT)
    table = jnp.asarray(table)
    undealing = jnp.asarray(dealing.T, jnp.bfloat16)
    dealing = jnp.asarray(dealing, jnp.bfloat16)

    own = pl.pallas_call(
        lambda *refs: prepare(cells, tiles, *refs),
        out_shape=jax.ShapeDtypeStruct((7, tiles, cells, LANES), jnp.float32),
        in_specs=[vmem] * 4,
        out_specs=vmem,
        compiler_params=params,
        cost_estimate=pl.CostEstimate(flops=10**9, bytes_accessed=10**7, transcendentals=0),
        name="prepare",
    )(start, depth, table, dealing)
    return pl.pallas_call(
        lambda *refs: kernel(cells, tiles, *refs),
        out_shape=jax.ShapeDtypeStruct((1, *start.shape), jnp.float32),
        in_specs=[vmem] * 6,
        out_specs=vmem,
        scratch_shapes=[pltpu.VMEM((tiles, wide, LANES), jnp.float32)] * 23,
        compiler_params=params,
        name="parareal",
    )(own, left, right, table, dealing, undealing)


def solution(mesh):
    return jax.shard_map(
        body,
        mesh=mesh,
        in_specs=(P(None, "lon", None), P("lon", None)),
        out_specs=P("tm", None, "lon", None),
        check_vma=False,
    )
```

time: 16.3 us -> 14.2 us (0.87)
  the two profiles are of different devices: /device:TPU:31 before, /device:TPU:27 now
where the time goes in v2:
time: 14.2 us; the launch traced here: 14 us
  Pallas kernels  6.59 us (46%)
  waiting for transfers between devices  2.73 us (19%)
  local copies, waits for them, and re-layouts  2.67 us (19%)
  starting transfers between devices  1.91 us (13%)
    pallas_call x1, Pallas kernels, body(): pl.pallas_call(lambda *refs: kernel(cells, tiles, *refs), out_shape=jax.S...  6.2 us
    ppermute x1, waiting for transfers between devices, body(): right = lax.ppermute(edge(0, HALO), 'lon', [(j, i) for i, j in ring])  2.52 us
    ppermute x1, starting transfers between devices, body(): left = lax.ppermute(edge(cells - HALO, cells), 'lon', ring)  1.85 us
    slice x1, local copies, waits for them, and re-layouts, edge(): start[:, low:high]  0.96 us
    unnamed x10, local copies, waits for them, and re-layouts  0.91 us
    broadcast_in_dim x1, local copies, waits for them, and re-layouts, edge(): depth[None, low:high]  0.78 us
    pallas_call x1, Pallas kernels, body(): pl.pallas_call(lambda *refs: prepare(cells, tiles, *refs), out_shape=jax....  0.39 us
  transfers between devices with their start and end apart: 2, of which 2 were waited for; matrix products, arithmetic and copies ran while one was open for 0% of the time, Pallas kernels for 3%

profile of v2, /device:TPU:27, one launch (start us, length us, event | category | flops | bytes accessed | tf_op | source)
XLA Modules:
  0.0 14.0 jit_solution(12446172542499701460)
XLA Ops:
  0.0 0.8 %slice_bitcast_fusion = (f32[1,12,512]{2,1,0:T(8,128)S(1)}, f32[1,12,512]{2,1,0:T(8,128)S(1)}) fusion(f32[32,512]{1,0:T(8,128)} %refs_1_.1), kind=kLoop, calls=%fused_computation.2 | loop fusion | bytes 98304 | tf_op jit(solution)/shard_map/broadcast_in_dim | solution.py:253
  0.8 1.0 %fusion = (f32[3,12,512]{2,1,0:T(8,128)S(1)}, f32[3,12,512]{2,1,0:T(8,128)S(1)}) fusion(f32[3,32,512]{2,1,0:T(8,128)} %refs_0_.1), kind=kLoop, calls=%fused_computation.4 | loop fusion | bytes 294912 | tf_op jit(solution)/shard_map/slice | solution.py:253
  1.7 0.0 copy-start
  1.8 1.9 %collective-permute-start = (f32[48,512]{1,0:T(8,128)S(1)}, f32[48,512]{1,0:T(8,128)S(1)}, u32[]{:S(2)}, u32[]{:S(2)}) collective-permute-start(f32[48,512]{1,0:T(8,128)S(1)} %reshape.6), channel_id=1, source_target_pairs={{0,1},{1,2},{2,3},{3,0},{4,5},{5,6},{6,7},{7,4},{8,9},{9,10},{10,1... | collective-permute-start | bytes 294920 | tf_op jit(solution)/shard_map/ppermute | solution.py:256
  3.6 0.0 copy-start.2
  3.7 0.0 copy-start.3
  3.7 0.0 copy-start.4
  3.7 0.0 copy-start.1
  3.7 0.1 collective-permute-start.1
  3.8 0.0 copy-done
  3.8 0.8 %copy-done.2 = f32[12,8,512]{2,1,0:T(8,128)S(1)} copy-done((f32[12,8,512]{2,1,0:T(8,128)S(1)}, f32[12,8,512]{2,1,0:T(8,128)}, u32[]{:S(2)}) %copy-start.2) | copy-done | bytes 196632
  4.6 0.1 copy-done.3
  4.7 0.0 copy-done.4
  4.7 0.4 %prepare.1.refs_0_ = f32[7,4,32,128]{3,2,1,0:T(8,128)S(1)} custom-call(f32[3,32,512]{2,1,0:T(8,128)S(1)} %copy-done.3, f32[32,512]{1,0:T(8,128)S(1)} %copy-done.4, f32[12,8,512]{2,1,0:T(8,128)S(1)} %copy-done.2, bf16[512,512]{1,0:T(8,128)(2,1)S(1)} %copy-done), custom_call_target="tpu_custom_call" | custom-call | flops 1000000000 | bytes 10000000 | tf_op jit(solution)/shard_map/prepare/pallas_call | solution.py:265
  5.1 0.2 %collective-permute-done.refs_1_ = f32[48,512]{1,0:T(8,128)S(1)} collective-permute-done((f32[48,512]{1,0:T(8,128)S(1)}, f32[48,512]{1,0:T(8,128)S(1)}, u32[]{:S(2)}, u32[]{:S(2)}) %collective-permute-start) | collective-permute-done | bytes 98336 | tf_op jit(solution)/shard_map/ppermute | solution.py:256
  5.3 2.5 %collective-permute-done.1.refs_2_ = f32[48,512]{1,0:T(8,128)S(1)} collective-permute-done((f32[48,512]{1,0:T(8,128)S(1)}, f32[48,512]{1,0:T(8,128)S(1)}, u32[]{:S(2)}, u32[]{:S(2)}) %collective-permute-start.1) | collective-permute-done | bytes 98336 | tf_op jit(solution)/shard_map/ppermute | solution.py:257
  7.8 0.0 copy-done.1
  7.8 6.2 %parareal.1 = f32[1,3,32,512]{3,2,1,0:T(8,128)} custom-call(f32[7,4,32,128]{3,2,1,0:T(8,128)S(1)} %prepare.1.refs_0_, f32[48,512]{1,0:T(8,128)S(1)} %collective-permute-done.refs_1_, f32[48,512]{1,0:T(8,128)S(1)} %collective-permute-done.1.refs_2_, f32[12,8,512]{2,1,0:T(8,128)S(1)} %copy-done.2, bf16[512,512]{1,0:T(8,128)(2,1)S(1)} %copy-done, ...), custom_call_target="tpu_custom_call" | custom-call | tf_op jit(solution)/shard_map/parareal/pallas_call | solution.py:274
  (4 shorter events, 0.0 us)
Async XLA Ops:
  1.7 2.0 %copy-start = (bf16[512,512]{1,0:T(8,128)(2,1)S(1)}, bf16[512,512]{1,0:T(8,128)(2,1)}, u32[]{:S(2)}) copy-start(bf16[512,512]{1,0:T(8,128)(2,1)} %constant.8.clone.refs_3_.refs_4_) | copy-start | bytes 1572868
  1.8 3.5 %collective-permute-start = (f32[48,512]{1,0:T(8,128)S(1)}, f32[48,512]{1,0:T(8,128)S(1)}, u32[]{:S(2)}, u32[]{:S(2)}) collective-permute-start(f32[48,512]{1,0:T(8,128)S(1)} %reshape.6), channel_id=1, source_target_pairs={{0,1},{1,2},{2,3},{3,0},{4,5},{5,6},{6,7},{7,4},{8,9},{9,10},{10,1... | collective-permute-start | bytes 294920 | tf_op jit(solution)/shard_map/ppermute | solution.py:256
  3.6 0.9 %copy-start.2 = (f32[12,8,512]{2,1,0:T(8,128)S(1)}, f32[12,8,512]{2,1,0:T(8,128)}, u32[]{:S(2)}) copy-start(f32[12,8,512]{2,1,0:T(8,128)} %constant.6.clone.refs_2_.refs_3_) | copy-start | bytes 589828
  3.7 1.0 %copy-start.3 = (f32[3,32,512]{2,1,0:T(8,128)S(1)}, f32[3,32,512]{2,1,0:T(8,128)}, u32[]{:S(2)}) copy-start(f32[3,32,512]{2,1,0:T(8,128)} %refs_0_.1) | copy-start | bytes 589828
  3.7 1.0 %copy-start.4 = (f32[32,512]{1,0:T(8,128)S(1)}, f32[32,512]{1,0:T(8,128)}, u32[]{:S(2)}) copy-start(f32[32,512]{1,0:T(8,128)} %refs_1_.1) | copy-start | bytes 196612
  3.7 4.1 %copy-start.1 = (bf16[512,512]{1,0:T(8,128)(2,1)S(1)}, bf16[512,512]{1,0:T(8,128)(2,1)}, u32[]{:S(2)}) copy-start(bf16[512,512]{1,0:T(8,128)(2,1)} %constant.7.clone.refs_5_) | copy-start | bytes 1572868
  3.7 4.1 %collective-permute-start.1 = (f32[48,512]{1,0:T(8,128)S(1)}, f32[48,512]{1,0:T(8,128)S(1)}, u32[]{:S(2)}, u32[]{:S(2)}) collective-permute-start(f32[48,512]{1,0:T(8,128)S(1)} %reshape.7), channel_id=1, source_target_pairs={{1,0},{2,1},{3,2},{0,3},{5,4},{6,5},{7,6},{4,7},{9,8},{10,9},{11,1... | collective-permute-start | bytes 294920 | tf_op jit(solution)/shard_map/ppermute | solution.py:257
